TPU v7x, 256 devices: a whole 4x4x8 slice. The times are simulated.
256 devices in a mesh: dp: 16 (over z, x_lo), ctx: 16 (over x_hi, y, core).
Axes of the slice: x: 4 (x_hi: 2, x_lo: 2; x = x_hi * 2 + x_lo), y: 4, z: 8, core: 2. Of those that a mesh axis runs over, the one named last changes fastest.
Arguments:
- normed: bfloat16 [16, 4096, 2048], P('dp', 'ctx'), may hold values from -21 to 21
- token_ids: int32 [16, 4096], P('dp', 'ctx'), may hold values from 0 to 128255
- block_order: int32 [16], replicated, may hold values from 0 to 15, each once
- master_weight: float32 [2048, 3072], P(('dp', 'ctx')), may hold values from -0.125 to 0.125
- weight_grad: float32 [2048, 3072], P(('dp', 'ctx')), may hold values from -6 to 6
- moment_one: float32 [2048, 3072], P(('dp', 'ctx')), may hold values from -4 to 4
- moment_two: float32 [2048, 3072], P(('dp', 'ctx')), may hold values from 0.1 to 3
Outputs:
- new_master: float32 [2048, 3072], P(('dp', 'ctx'))
- new_moment_one: float32 [2048, 3072], P(('dp', 'ctx'))
- new_moment_two: float32 [2048, 3072], P(('dp', 'ctx'))
- attended: bfloat16 [16, 4096, 2048], P('dp', 'ctx')
All inputs are finite; a program needn't handle non-finite values.
Results may differ from a plain program's by a relative error of at most 0.008.
The roundings to bfloat16 on the way count: a program that leaves them out, or rounds other values in their place, can miss the bound.
Values may be sent and summed in bfloat16 or wider, within the bound.
A program may use at most 64 MiB of HBM per device.

v0:
```python
import jax
import jax.numpy as jnp
from jax import lax
from jax.sharding import PartitionSpec as P

HQ = 16
HK = 4
DH = 128
GROUP = 4
beta_one = 0.9
beta_two = 0.95
adam_step = 10.0
learn_rate = 0.0003
decay_rate = 0.1
adam_eps = 1e-08
rope_theta = 500000.0
masked_score = -1e30


def passed_along(x, axis, by):
    count = lax.axis_size(axis)
    return lax.ppermute(x, axis, [(i, (i + by) % count) for i in range(count)])


def adam_update(master_weight, weight_grad, moment_one, moment_two):
    fresh_one = beta_one * moment_one + (1.0 - beta_one) * weight_grad
    fresh_two = beta_two * moment_two + (1.0 - beta_two) * weight_grad * weight_grad
    fix_one = 1.0 - beta_one**adam_step
    fix_two = 1.0 - beta_two**adam_step
    step_size = fresh_one / fix_one / (jnp.sqrt(fresh_two / fix_two) + adam_eps)
    fresh_master = master_weight - learn_rate * (step_size + decay_rate * master_weight)
    return (fresh_master, fresh_one, fresh_two)


def rotate(values, positions):
    half_dim = values.shape[-1] // 2
    frequency = rope_theta ** (-2.0 * jnp.arange(half_dim, dtype=jnp.float32) / values.shape[-1])
    angles = positions.astype(jnp.float32)[:, None] * frequency[None, :]
    cosine = jnp.cos(angles)[:, None, :]
    sine_part = jnp.sin(angles)[:, None, :]
    first_half = values[..., :half_dim]
    second_half = values[..., half_dim:]
    return jnp.concatenate(
        [
            first_half * cosine - second_half * sine_part,
            second_half * cosine + first_half * sine_part,
        ],
        -1,
    )


def local(normed, token_ids, block_order, master_weight, weight_grad, moment_one, moment_two):
    new_master, new_moment_one, new_moment_two = adam_update(
        master_weight, weight_grad, moment_one, moment_two
    )
    fresh_weight = new_master.astype(jnp.bfloat16)
    tok_rows = normed[0]
    block_len = tok_rows.shape[0]
    projected = jnp.dot(
        tok_rows,
        lax.all_gather(fresh_weight, ("dp", "ctx"), axis=0, tiled=True),
        preferred_element_type=jnp.float32,
    )
    place = lax.axis_index("ctx")
    place_count = lax.axis_size("ctx")
    local_idx = jnp.arange(block_len, dtype=jnp.int32)
    my_block = block_order[place]
    positions = my_block * block_len + local_idx
    doc_gap = block_len * place_count // 2
    marks = jnp.where(token_ids[0] % doc_gap == 0, positions, 0)
    last_mark = jnp.max(marks)
    all_marks = lax.all_gather(last_mark[None], "ctx", axis=0, tiled=True)
    prior_mark = jnp.max(jnp.where(block_order < my_block, all_marks, 0))
    doc_start = jnp.maximum(lax.cummax(marks, axis=0), prior_mark)
    queries = rotate(projected[:, : HQ * DH].reshape(block_len, HQ, DH), positions).astype(
        jnp.bfloat16
    )
    key_rows = rotate(
        projected[:, HQ * DH : (HQ + HK) * DH].reshape(block_len, HK, DH), positions
    ).astype(jnp.bfloat16)
    value_rows = projected[:, (HQ + HK) * DH :].astype(jnp.bfloat16)
    key_block = jnp.concatenate([key_rows.reshape(block_len, HK * DH), value_rows], 1)
    score_scale = DH ** (-0.5)

    def attend_head(carry, kv_head, key_part, value_part, key_pos):
        run_max, run_sum, run_acc = carry
        group_q = queries[:, kv_head * GROUP : (kv_head + 1) * GROUP, :]
        scores = (
            jnp.einsum("qjd,kd->jqk", group_q, key_part, preferred_element_type=jnp.float32)
            * score_scale
        )
        allowed = (key_pos[None, :] <= positions[:, None]) & (
            key_pos[None, :] >= doc_start[:, None]
        )
        scores = jnp.where(allowed[None], scores, masked_score)
        new_max = jnp.maximum(run_max, jnp.max(scores, -1))
        weights = jnp.where(allowed[None], jnp.exp(scores - new_max[..., None]), 0.0)
        factor = jnp.exp(run_max - new_max)
        run_sum = run_sum * factor + jnp.sum(weights, -1)
        run_acc = run_acc * factor[..., None] + jnp.einsum(
            "jqk,kd->jqd",
            weights.astype(jnp.bfloat16),
            value_part,
            preferred_element_type=jnp.float32,
        )
        return (new_max, run_sum, run_acc)

    def attend_block(carries, moving, source, head_list):
        key_pos = block_order[source] * block_len + local_idx
        head_count = len(head_list)
        updated = list(carries)
        for slot, kv_head in enumerate(head_list):
            key_part = moving[:, slot * DH : (slot + 1) * DH]
            value_part = moving[:, (head_count + slot) * DH : (head_count + slot + 1) * DH]
            updated[kv_head] = attend_head(carries[kv_head], kv_head, key_part, value_part, key_pos)
        return tuple(updated)

    start_state = (
        jnp.full((GROUP, block_len), masked_score, jnp.float32),
        jnp.zeros((GROUP, block_len), jnp.float32),
        jnp.zeros((GROUP, block_len, DH), jnp.float32),
    )
    carries = tuple((start_state for kv_head in range(HK)))
    every_head = list(range(HK))
    carries = attend_block(carries, key_block, place, every_head)

    def one_step(step_idx, state):
        held, moving = state
        moving = passed_along(moving, "ctx", 1)
        source = (place - step_idx - 1) % place_count
        return (attend_block(held, moving, source, every_head), moving)

    carries, unused_block = lax.fori_loop(0, place_count - 1, one_step, (carries, key_block))
    head_outputs = []
    for kv_head in range(HK):
        run_max, run_sum, run_acc = carries[kv_head]
        normalized = run_acc / run_sum[..., None]
        head_outputs.append(jnp.transpose(normalized, (1, 0, 2)).reshape(block_len, GROUP * DH))
    attended = jnp.concatenate(head_outputs, 1).astype(jnp.bfloat16)
    return (new_master, new_moment_one, new_moment_two, attended[None])


def solution(mesh):
    in_specs = (
        P("dp", "ctx", None),
        P("dp", "ctx"),
        P(),
        P(("dp", "ctx"), None),
        P(("dp", "ctx"), None),
        P(("dp", "ctx"), None),
        P(("dp", "ctx"), None),
    )
    out_specs = (
        P(("dp", "ctx"), None),
        P(("dp", "ctx"), None),
        P(("dp", "ctx"), None),
        P("dp", "ctx", None),
    )
    return jax.shard_map(local, mesh=mesh, in_specs=in_specs, out_specs=out_specs, check_vma=False)
```

profile of v0, /device:TPU:32, one launch (start us, length us, event | category | flops | bytes accessed | tf_op | source)
XLA Modules:
  0.0 757.4 jit_solution(6095916171341330654)
XLA Ops:
  17.4 14.1 %all-reduce = s32[16]{0:T(128)S(1)} all-reduce(s32[16]{0:T(128)S(1)} %dynamic-update-slice), channel_id=1, replica_groups=mesh['dp'=16,'ctx'=16] {'ctx'}, use_global_device_ids=true, to_apply=%add | all-reduce | flops 16 | bytes 128
  34.5 402.0 %all-gather.2.cloned.1.call-done = bf16[2048,3072]{1,0:T(8,128)(2,1)} async-done(((bf16[8,3072]{1,0:T(8,128)(2,1)}), bf16[2048,3072]{1,0:T(8,128)(2,1)}) %all-gather.2.cloned.1.call-update) | async-done | bytes 12582928 | tf_op jit(solution)/shard_map/all_gather | solution.py:61
  436.5 9.7 %fusion.118 = (bf16[256,3072]{0,1:T(8,128)(2,1)}, f32[256,3072]{0,1:T(8,128)S(1)}) fusion(bf16[2048,3072]{1,0:T(8,128)(2,1)} %all-gather.2.cloned.1.call-done, bf16[1,256,2048]{2,1,0:T(8,128)(2,1)S(1)} %copy-done), kind=kOutput, calls=%fused_computation.202 | convolution fusion | flops 3222011904 | bytes 18350080 | tf_op jit(solution)/shard_map/dot_general | solution.py:59
  450.5 3.2 copy.111
  454.8 2.2 add_convert_fusion
  462.4 2.1 convolution_add_fusion.6
  464.5 2.1 convolution_add_fusion.5
  466.6 2.1 convolution_add_fusion.4
  469.8 276.4 %while.40 = (s32[]{:T(128)}, f32[4,256]{1,0:T(4,128)S(1)}, f32[4,256]{1,0:T(4,128)S(1)}, f32[4,256,128]{2,1,0:T(8,128)S(1)}, f32[4,256]{1,0:T(4,128)S(1)}, /*ind...) while((s32[]{:T(128)}, f32[4,256]{1,0:T(4,128)S(1)}, ...), condition=%wide.region_21.22_spmd.clone, body=%wide.region_12.21_spmd.clone.sunk | while | flops 547561984 | bytes 35001972 | solution.py:133
  471.1 11.1 %collective-permute-done = bf16[256,1024]{1,0:T(8,128)(2,1)S(1)} collective-permute-done((bf16[256,1024]{1,0:T(8,128)(2,1)}, bf16[256,1024]{1,0:T(8,128)(2,1)S(1)}, u32[]{:S(2)}, u32[]{:S(2)}) %collective-permute-start) | collective-permute-done | bytes 524320 | tf_op jit(solution)/shard_map/while/body/eval_jaxpr/ppermute | solution.py:22
  489.6 11.1 %collective-permute-done = bf16[256,1024]{1,0:T(8,128)(2,1)S(1)} collective-permute-done((bf16[256,1024]{1,0:T(8,128)(2,1)}, bf16[256,1024]{1,0:T(8,128)(2,1)S(1)}, u32[]{:S(2)}, u32[]{:S(2)}) %collective-permute-start) | collective-permute-done | bytes 524320 | tf_op jit(solution)/shard_map/while/body/eval_jaxpr/ppermute | solution.py:22
  508.0 11.1 %collective-permute-done = bf16[256,1024]{1,0:T(8,128)(2,1)S(1)} collective-permute-done((bf16[256,1024]{1,0:T(8,128)(2,1)}, bf16[256,1024]{1,0:T(8,128)(2,1)S(1)}, u32[]{:S(2)}, u32[]{:S(2)}) %collective-permute-start) | collective-permute-done | bytes 524320 | tf_op jit(solution)/shard_map/while/body/eval_jaxpr/ppermute | solution.py:22
  526.4 11.1 %collective-permute-done = bf16[256,1024]{1,0:T(8,128)(2,1)S(1)} collective-permute-done((bf16[256,1024]{1,0:T(8,128)(2,1)}, bf16[256,1024]{1,0:T(8,128)(2,1)S(1)}, u32[]{:S(2)}, u32[]{:S(2)}) %collective-permute-start) | collective-permute-done | bytes 524320 | tf_op jit(solution)/shard_map/while/body/eval_jaxpr/ppermute | solution.py:22
  544.8 11.1 %collective-permute-done = bf16[256,1024]{1,0:T(8,128)(2,1)S(1)} collective-permute-done((bf16[256,1024]{1,0:T(8,128)(2,1)}, bf16[256,1024]{1,0:T(8,128)(2,1)S(1)}, u32[]{:S(2)}, u32[]{:S(2)}) %collective-permute-start) | collective-permute-done | bytes 524320 | tf_op jit(solution)/shard_map/while/body/eval_jaxpr/ppermute | solution.py:22
  563.3 11.1 %collective-permute-done = bf16[256,1024]{1,0:T(8,128)(2,1)S(1)} collective-permute-done((bf16[256,1024]{1,0:T(8,128)(2,1)}, bf16[256,1024]{1,0:T(8,128)(2,1)S(1)}, u32[]{:S(2)}, u32[]{:S(2)}) %collective-permute-start) | collective-permute-done | bytes 524320 | tf_op jit(solution)/shard_map/while/body/eval_jaxpr/ppermute | solution.py:22
  581.7 11.1 %collective-permute-done = bf16[256,1024]{1,0:T(8,128)(2,1)S(1)} collective-permute-done((bf16[256,1024]{1,0:T(8,128)(2,1)}, bf16[256,1024]{1,0:T(8,128)(2,1)S(1)}, u32[]{:S(2)}, u32[]{:S(2)}) %collective-permute-start) | collective-permute-done | bytes 524320 | tf_op jit(solution)/shard_map/while/body/eval_jaxpr/ppermute | solution.py:22
  600.1 11.1 %collective-permute-done = bf16[256,1024]{1,0:T(8,128)(2,1)S(1)} collective-permute-done((bf16[256,1024]{1,0:T(8,128)(2,1)}, bf16[256,1024]{1,0:T(8,128)(2,1)S(1)}, u32[]{:S(2)}, u32[]{:S(2)}) %collective-permute-start) | collective-permute-done | bytes 524320 | tf_op jit(solution)/shard_map/while/body/eval_jaxpr/ppermute | solution.py:22
  618.5 11.1 %collective-permute-done = bf16[256,1024]{1,0:T(8,128)(2,1)S(1)} collective-permute-done((bf16[256,1024]{1,0:T(8,128)(2,1)}, bf16[256,1024]{1,0:T(8,128)(2,1)S(1)}, u32[]{:S(2)}, u32[]{:S(2)}) %collective-permute-start) | collective-permute-done | bytes 524320 | tf_op jit(solution)/shard_map/while/body/eval_jaxpr/ppermute | solution.py:22
  637.0 11.1 %collective-permute-done = bf16[256,1024]{1,0:T(8,128)(2,1)S(1)} collective-permute-done((bf16[256,1024]{1,0:T(8,128)(2,1)}, bf16[256,1024]{1,0:T(8,128)(2,1)S(1)}, u32[]{:S(2)}, u32[]{:S(2)}) %collective-permute-start) | collective-permute-done | bytes 524320 | tf_op jit(solution)/shard_map/while/body/eval_jaxpr/ppermute | solution.py:22
  655.4 11.1 %collective-permute-done = bf16[256,1024]{1,0:T(8,128)(2,1)S(1)} collective-permute-done((bf16[256,1024]{1,0:T(8,128)(2,1)}, bf16[256,1024]{1,0:T(8,128)(2,1)S(1)}, u32[]{:S(2)}, u32[]{:S(2)}) %collective-permute-start) | collective-permute-done | bytes 524320 | tf_op jit(solution)/shard_map/while/body/eval_jaxpr/ppermute | solution.py:22
  673.8 11.1 %collective-permute-done = bf16[256,1024]{1,0:T(8,128)(2,1)S(1)} collective-permute-done((bf16[256,1024]{1,0:T(8,128)(2,1)}, bf16[256,1024]{1,0:T(8,128)(2,1)S(1)}, u32[]{:S(2)}, u32[]{:S(2)}) %collective-permute-start) | collective-permute-done | bytes 524320 | tf_op jit(solution)/shard_map/while/body/eval_jaxpr/ppermute | solution.py:22
  692.3 11.1 %collective-permute-done = bf16[256,1024]{1,0:T(8,128)(2,1)S(1)} collective-permute-done((bf16[256,1024]{1,0:T(8,128)(2,1)}, bf16[256,1024]{1,0:T(8,128)(2,1)S(1)}, u32[]{:S(2)}, u32[]{:S(2)}) %collective-permute-start) | collective-permute-done | bytes 524320 | tf_op jit(solution)/shard_map/while/body/eval_jaxpr/ppermute | solution.py:22
  710.7 11.1 %collective-permute-done = bf16[256,1024]{1,0:T(8,128)(2,1)S(1)} collective-permute-done((bf16[256,1024]{1,0:T(8,128)(2,1)}, bf16[256,1024]{1,0:T(8,128)(2,1)S(1)}, u32[]{:S(2)}, u32[]{:S(2)}) %collective-permute-start) | collective-permute-done | bytes 524320 | tf_op jit(solution)/shard_map/while/body/eval_jaxpr/ppermute | solution.py:22
  729.1 11.1 %collective-permute-done = bf16[256,1024]{1,0:T(8,128)(2,1)S(1)} collective-permute-done((bf16[256,1024]{1,0:T(8,128)(2,1)}, bf16[256,1024]{1,0:T(8,128)(2,1)S(1)}, u32[]{:S(2)}, u32[]{:S(2)}) %collective-permute-start) | collective-permute-done | bytes 524320 | tf_op jit(solution)/shard_map/while/body/eval_jaxpr/ppermute | solution.py:22
  (621 shorter events, 127.0 us)
Async XLA Ops:
  7.2 429.3 %copy-start = (bf16[1,256,2048]{2,1,0:T(8,128)(2,1)S(1)}, bf16[1,256,2048]{2,1,0:T(8,128)(2,1)}, u32[]{:S(2)}) copy-start(bf16[1,256,2048]{2,1,0:T(8,128)(2,1)} %param.9) | copy-start | bytes 3145732
  7.2 429.3 %all-gather.2.cloned.1.call-start = ((), (), s32[]{:S(2)}) async-start(), calls=%async_computation | async-start | bytes 12632064 | tf_op jit(solution)/shard_map/all_gather | solution.py:61
  466.6 3.2 copy-start.9
  469.8 12.4 %collective-permute-start = (bf16[256,1024]{1,0:T(8,128)(2,1)}, bf16[256,1024]{1,0:T(8,128)(2,1)S(1)}, u32[]{:S(2)}, u32[]{:S(2)}) collective-permute-start(bf16[256,1024]{1,0:T(8,128)(2,1)} %get-tuple-element.873), channel_id=1, source_target_pairs={{0,1},{1,2},{2,3},{3,4},{4,5},{5,6},{6,7},{7,8},{8,9},{9,10},{10,1... | collective-permute-start | bytes 1572872 | tf_op jit(solution)/shard_map/while/body/eval_jaxpr/ppermute | solution.py:22
  488.2 12.4 %collective-permute-start = (bf16[256,1024]{1,0:T(8,128)(2,1)}, bf16[256,1024]{1,0:T(8,128)(2,1)S(1)}, u32[]{:S(2)}, u32[]{:S(2)}) collective-permute-start(bf16[256,1024]{1,0:T(8,128)(2,1)} %get-tuple-element.873), channel_id=1, source_target_pairs={{0,1},{1,2},{2,3},{3,4},{4,5},{5,6},{6,7},{7,8},{8,9},{9,10},{10,1... | collective-permute-start | bytes 1572872 | tf_op jit(solution)/shard_map/while/body/eval_jaxpr/ppermute | solution.py:22
  502.7 1.4 copy-start.1
  506.6 12.4 %collective-permute-start = (bf16[256,1024]{1,0:T(8,128)(2,1)}, bf16[256,1024]{1,0:T(8,128)(2,1)S(1)}, u32[]{:S(2)}, u32[]{:S(2)}) collective-permute-start(bf16[256,1024]{1,0:T(8,128)(2,1)} %get-tuple-element.873), channel_id=1, source_target_pairs={{0,1},{1,2},{2,3},{3,4},{4,5},{5,6},{6,7},{7,8},{8,9},{9,10},{10,1... | collective-permute-start | bytes 1572872 | tf_op jit(solution)/shard_map/while/body/eval_jaxpr/ppermute | solution.py:22
  525.0 12.4 %collective-permute-start = (bf16[256,1024]{1,0:T(8,128)(2,1)}, bf16[256,1024]{1,0:T(8,128)(2,1)S(1)}, u32[]{:S(2)}, u32[]{:S(2)}) collective-permute-start(bf16[256,1024]{1,0:T(8,128)(2,1)} %get-tuple-element.873), channel_id=1, source_target_pairs={{0,1},{1,2},{2,3},{3,4},{4,5},{5,6},{6,7},{7,8},{8,9},{9,10},{10,1... | collective-permute-start | bytes 1572872 | tf_op jit(solution)/shard_map/while/body/eval_jaxpr/ppermute | solution.py:22
  543.5 12.4 %collective-permute-start = (bf16[256,1024]{1,0:T(8,128)(2,1)}, bf16[256,1024]{1,0:T(8,128)(2,1)S(1)}, u32[]{:S(2)}, u32[]{:S(2)}) collective-permute-start(bf16[256,1024]{1,0:T(8,128)(2,1)} %get-tuple-element.873), channel_id=1, source_target_pairs={{0,1},{1,2},{2,3},{3,4},{4,5},{5,6},{6,7},{7,8},{8,9},{9,10},{10,1... | collective-permute-start | bytes 1572872 | tf_op jit(solution)/shard_map/while/body/eval_jaxpr/ppermute | solution.py:22
  561.9 12.4 %collective-permute-start = (bf16[256,1024]{1,0:T(8,128)(2,1)}, bf16[256,1024]{1,0:T(8,128)(2,1)S(1)}, u32[]{:S(2)}, u32[]{:S(2)}) collective-permute-start(bf16[256,1024]{1,0:T(8,128)(2,1)} %get-tuple-element.873), channel_id=1, source_target_pairs={{0,1},{1,2},{2,3},{3,4},{4,5},{5,6},{6,7},{7,8},{8,9},{9,10},{10,1... | collective-permute-start | bytes 1572872 | tf_op jit(solution)/shard_map/while/body/eval_jaxpr/ppermute | solution.py:22
  580.3 12.4 %collective-permute-start = (bf16[256,1024]{1,0:T(8,128)(2,1)}, bf16[256,1024]{1,0:T(8,128)(2,1)S(1)}, u32[]{:S(2)}, u32[]{:S(2)}) collective-permute-start(bf16[256,1024]{1,0:T(8,128)(2,1)} %get-tuple-element.873), channel_id=1, source_target_pairs={{0,1},{1,2},{2,3},{3,4},{4,5},{5,6},{6,7},{7,8},{8,9},{9,10},{10,1... | collective-permute-start | bytes 1572872 | tf_op jit(solution)/shard_map/while/body/eval_jaxpr/ppermute | solution.py:22
  598.7 12.4 %collective-permute-start = (bf16[256,1024]{1,0:T(8,128)(2,1)}, bf16[256,1024]{1,0:T(8,128)(2,1)S(1)}, u32[]{:S(2)}, u32[]{:S(2)}) collective-permute-start(bf16[256,1024]{1,0:T(8,128)(2,1)} %get-tuple-element.873), channel_id=1, source_target_pairs={{0,1},{1,2},{2,3},{3,4},{4,5},{5,6},{6,7},{7,8},{8,9},{9,10},{10,1... | collective-permute-start | bytes 1572872 | tf_op jit(solution)/shard_map/while/body/eval_jaxpr/ppermute | solution.py:22
  613.3 1.4 copy-start.1
  617.2 12.4 %collective-permute-start = (bf16[256,1024]{1,0:T(8,128)(2,1)}, bf16[256,1024]{1,0:T(8,128)(2,1)S(1)}, u32[]{:S(2)}, u32[]{:S(2)}) collective-permute-start(bf16[256,1024]{1,0:T(8,128)(2,1)} %get-tuple-element.873), channel_id=1, source_target_pairs={{0,1},{1,2},{2,3},{3,4},{4,5},{5,6},{6,7},{7,8},{8,9},{9,10},{10,1... | collective-permute-start | bytes 1572872 | tf_op jit(solution)/shard_map/while/body/eval_jaxpr/ppermute | solution.py:22
  631.7 1.4 copy-start.1
  635.6 12.4 %collective-permute-start = (bf16[256,1024]{1,0:T(8,128)(2,1)}, bf16[256,1024]{1,0:T(8,128)(2,1)S(1)}, u32[]{:S(2)}, u32[]{:S(2)}) collective-permute-start(bf16[256,1024]{1,0:T(8,128)(2,1)} %get-tuple-element.873), channel_id=1, source_target_pairs={{0,1},{1,2},{2,3},{3,4},{4,5},{5,6},{6,7},{7,8},{8,9},{9,10},{10,1... | collective-permute-start | bytes 1572872 | tf_op jit(solution)/shard_map/while/body/eval_jaxpr/ppermute | solution.py:22
  654.0 12.4 %collective-permute-start = (bf16[256,1024]{1,0:T(8,128)(2,1)}, bf16[256,1024]{1,0:T(8,128)(2,1)S(1)}, u32[]{:S(2)}, u32[]{:S(2)}) collective-permute-start(bf16[256,1024]{1,0:T(8,128)(2,1)} %get-tuple-element.873), channel_id=1, source_target_pairs={{0,1},{1,2},{2,3},{3,4},{4,5},{5,6},{6,7},{7,8},{8,9},{9,10},{10,1... | collective-permute-start | bytes 1572872 | tf_op jit(solution)/shard_map/while/body/eval_jaxpr/ppermute | solution.py:22
  672.4 12.4 %collective-permute-start = (bf16[256,1024]{1,0:T(8,128)(2,1)}, bf16[256,1024]{1,0:T(8,128)(2,1)S(1)}, u32[]{:S(2)}, u32[]{:S(2)}) collective-permute-start(bf16[256,1024]{1,0:T(8,128)(2,1)} %get-tuple-element.873), channel_id=1, source_target_pairs={{0,1},{1,2},{2,3},{3,4},{4,5},{5,6},{6,7},{7,8},{8,9},{9,10},{10,1... | collective-permute-start | bytes 1572872 | tf_op jit(solution)/shard_map/while/body/eval_jaxpr/ppermute | solution.py:22
  690.9 12.4 %collective-permute-start = (bf16[256,1024]{1,0:T(8,128)(2,1)}, bf16[256,1024]{1,0:T(8,128)(2,1)S(1)}, u32[]{:S(2)}, u32[]{:S(2)}) collective-permute-start(bf16[256,1024]{1,0:T(8,128)(2,1)} %get-tuple-element.873), channel_id=1, source_target_pairs={{0,1},{1,2},{2,3},{3,4},{4,5},{5,6},{6,7},{7,8},{8,9},{9,10},{10,1... | collective-permute-start | bytes 1572872 | tf_op jit(solution)/shard_map/while/body/eval_jaxpr/ppermute | solution.py:22
  709.3 12.4 %collective-permute-start = (bf16[256,1024]{1,0:T(8,128)(2,1)}, bf16[256,1024]{1,0:T(8,128)(2,1)S(1)}, u32[]{:S(2)}, u32[]{:S(2)}) collective-permute-start(bf16[256,1024]{1,0:T(8,128)(2,1)} %get-tuple-element.873), channel_id=1, source_target_pairs={{0,1},{1,2},{2,3},{3,4},{4,5},{5,6},{6,7},{7,8},{8,9},{9,10},{10,1... | collective-permute-start | bytes 1572872 | tf_op jit(solution)/shard_map/while/body/eval_jaxpr/ppermute | solution.py:22
  727.7 12.4 %collective-permute-start = (bf16[256,1024]{1,0:T(8,128)(2,1)}, bf16[256,1024]{1,0:T(8,128)(2,1)S(1)}, u32[]{:S(2)}, u32[]{:S(2)}) collective-permute-start(bf16[256,1024]{1,0:T(8,128)(2,1)} %get-tuple-element.873), channel_id=1, source_target_pairs={{0,1},{1,2},{2,3},{3,4},{4,5},{5,6},{6,7},{7,8},{8,9},{9,10},{10,1... | collective-permute-start | bytes 1572872 | tf_op jit(solution)/shard_map/while/body/eval_jaxpr/ppermute | solution.py:22
  742.3 1.4 copy-start.1
  746.1 1.7 copy-start.6
  746.2 2.2 copy-start.3
  (86 other events, 88.6 us)
Sparse Core Ops, SparseCore 0:
  10.4 426.0 all-gather.1
where the time goes:
time: 759 us; the launch traced here: 757 us
  waiting for transfers between devices  568 us (75%)
  matrix products  69.1 us (9%)
  local copies, waits for them, and re-layouts  49.7 us (7%)
  other arithmetic  29.4 us (4%)
  between operations  14.9 us (2%)
  blocking collectives  14.1 us (2%)
  loops' own time  12.3 us (2%)
    all_gather x1, waiting for transfers between devices, local(): lax.all_gather(fresh_weight, ('dp', 'ctx'), axis=0, tiled=True)  402 us
    ppermute x15, waiting for transfers between devices, passed_along(): return lax.ppermute(x, axis, [(i, (i + by) % count) for i in range(count)])  166 us
    dot_general x64, matrix products, attend_head(): jnp.einsum('jqk,kd->jqd', weights.astype(jnp.bfloat16), value_part, prefe...  38.3 us
    while x255, local copies, waits for them, and re-layouts  24.8 us
    dot_general x64, matrix products, attend_head(): jnp.einsum('qjd,kd->jqk', group_q, key_part, preferred_element_type=jnp.f...  21.1 us
  transfers between devices with their start and end apart: 16, of which 16 were waited for; matrix products, arithmetic and copies ran while one was open for 3% of the time, Pallas kernels for 0%

commit v1 on v0

--- a/solution.py
+++ b/solution.py
@@ -1,3 +1,4 @@
+import functools
 import jax
 import jax.numpy as jnp
 from jax import lax
@@ -15,6 +16,15 @@
 adam_eps = 1e-08
 rope_theta = 500000.0
 masked_score = -1e30
+
+
+def stacks_all_track(x0, axis_k):
+    all_rows = jnp.stack(tuple((x0 for _ in range(lax.axis_size(("dp", "ctx"))))))
+    formed = lax.all_to_all(all_rows, axis_name=("dp", "ctx"), split_axis=0, concat_axis=0)
+    return jnp.concatenate(formed, axis=axis_k)
+
+
+figure_extend = functools.partial(stacks_all_track, axis_k=0)
 
 
 def passed_along(x, axis, by):
@@ -56,11 +66,7 @@
     fresh_weight = new_master.astype(jnp.bfloat16)
     tok_rows = normed[0]
     block_len = tok_rows.shape[0]
-    projected = jnp.dot(
-        tok_rows,
-        lax.all_gather(fresh_weight, ("dp", "ctx"), axis=0, tiled=True),
-        preferred_element_type=jnp.float32,
-    )
+    projected = jnp.dot(tok_rows, figure_extend(fresh_weight), preferred_element_type=jnp.float32)
     place = lax.axis_index("ctx")
     place_count = lax.axis_size("ctx")
     local_idx = jnp.arange(block_len, dtype=jnp.int32)

time: 759 us -> 617 us (0.81)
  waiting for transfers between devices: 568 us -> 400 us
  blocking collectives: 14.1 us -> 35.9 us
  starting transfers between devices: 0.08 us -> 15.3 us
  between operations: 14.9 us -> 1.57 us
    all_gather x1 -> x0, waiting for transfers between devices: 402 us -> none  [local(): lax.all_gather(fresh_weight, ('dp', 'ctx'), axis=0, tiled=True)]
    all_to_all x0 -> x1, waiting for transfers between devices: none -> 234 us  [stacks_all_track(): lax.all_to_all(all_rows, axis_name=('dp', 'ctx'), split_axis=0, concat_ax...]
    unnamed x1, blocking collectives: 14.1 us -> 35.9 us
    all_to_all x0 -> x1, starting transfers between devices: none -> 15.3 us  [stacks_all_track(): lax.all_to_all(all_rows, axis_name=('dp', 'ctx'), split_axis=0, concat_ax...]
where the time goes in v1:
time: 617 us; the launch traced here: 616 us
  waiting for transfers between devices  400 us (65%)
  matrix products  69.1 us (11%)
  local copies, waits for them, and re-layouts  54.5 us (9%)
  blocking collectives  35.9 us (6%)
  other arithmetic  27.5 us (4%)
  starting transfers between devices  15.3 us (2%)
  loops' own time  12.3 us (2%)
    all_to_all x1, waiting for transfers between devices, stacks_all_track(): lax.all_to_all(all_rows, axis_name=('dp', 'ctx'), split_axis=0, concat_ax...  234 us
    ppermute x15, waiting for transfers between devices, passed_along(): return lax.ppermute(x, axis, [(i, (i + by) % count) for i in range(count)])  166 us
    dot_general x64, matrix products, attend_head(): jnp.einsum('jqk,kd->jqd', weights.astype(jnp.bfloat16), value_part, prefe...  38.3 us
    unnamed x1, blocking collectives  35.9 us
    while x255, local copies, waits for them, and re-layouts  24.8 us
    dot_general x64, matrix products, attend_head(): jnp.einsum('qjd,kd->jqk', group_q, key_part, preferred_element_type=jnp.f...  21.1 us
    all_to_all x1, starting transfers between devices, stacks_all_track(): lax.all_to_all(all_rows, axis_name=('dp', 'ctx'), split_axis=0, concat_ax...  15.3 us
  transfers between devices with their start and end apart: 16, of which 16 were waited for; matrix products, arithmetic and copies ran while one was open for 3% of the time, Pallas kernels for 0%

profile of v1, /device:TPU:32, one launch (start us, length us, event | category | flops | bytes accessed | tf_op | source)
XLA Modules:
  0.0 615.9 jit_solution(7038033841974025035)
XLA Ops:
  2.5 6.1 stack.2
  8.6 15.3 %all-to-all-start = ((bf16[256,8,3072]{2,1,0:T(8,128)(2,1)}), bf16[256,8,3072]{2,1,0:T(8,128)(2,1)}, u32[]{:S(2)}, u32[]{:S(2)}) async-start(bf16[256,8,3072]{2,1,0:T(8,128)(2,1)} %stack.2), calls=%async_computation | async-start | bytes 25165824 | tf_op jit(solution)/shard_map/all_to_all | solution.py:23
  29.6 35.9 %all-reduce = s32[16]{0:T(128)S(1)} all-reduce(s32[16]{0:T(128)S(1)} %dynamic-update-slice), channel_id=1, replica_groups=mesh['dp'=16,'ctx'=16] {'ctx'}, use_global_device_ids=true, to_apply=%add | all-reduce | flops 16 | bytes 128
  67.9 234.0 %all-to-all-done = bf16[256,8,3072]{2,1,0:T(8,128)(2,1)} async-done(((bf16[256,8,3072]{2,1,0:T(8,128)(2,1)}), bf16[256,8,3072]{2,1,0:T(8,128)(2,1)}, u32[]{:S(2)}, u32[]{:S(2)}) %all-to-all-start) | async-done | bytes 12582944 | tf_op jit(solution)/shard_map/all_to_all | solution.py:23
  301.9 9.7 %fusion.123 = (bf16[256,3072]{0,1:T(8,128)(2,1)}, f32[256,3072]{0,1:T(8,128)S(1)}) fusion(bf16[1,256,2048]{2,1,0:T(8,128)(2,1)S(1)} %copy-done, bf16[256,8,3072]{2,1,0:T(8,128)(2,1)} %all-to-all-done), kind=kOutput, calls=%fused_computation.204 | convolution fusion | flops 3222011904 | bytes 18350080 | tf_op jit(solution)/shard_map/dot_general | solution.py:69
  315.9 3.2 copy.111
  320.2 2.2 add_convert_fusion
  332.0 2.1 convolution_add_fusion.4
  335.1 276.4 %while.40 = (s32[]{:T(128)}, f32[4,256]{1,0:T(4,128)S(1)}, f32[4,256]{1,0:T(4,128)S(1)}, f32[4,256,128]{2,1,0:T(8,128)S(1)}, f32[4,256]{1,0:T(4,128)S(1)}, /*ind...) while((s32[]{:T(128)}, f32[4,256]{1,0:T(4,128)S(1)}, ...), condition=%wide.region_21.22_spmd.clone, body=%wide.region_12.21_spmd.clone.sunk | while | flops 547561984 | bytes 35001972 | solution.py:139
  336.5 11.1 %collective-permute-done = bf16[256,1024]{1,0:T(8,128)(2,1)S(1)} collective-permute-done((bf16[256,1024]{1,0:T(8,128)(2,1)}, bf16[256,1024]{1,0:T(8,128)(2,1)S(1)}, u32[]{:S(2)}, u32[]{:S(2)}) %collective-permute-start) | collective-permute-done | bytes 524320 | tf_op jit(solution)/shard_map/while/body/eval_jaxpr/ppermute | solution.py:32
  354.9 11.1 %collective-permute-done = bf16[256,1024]{1,0:T(8,128)(2,1)S(1)} collective-permute-done((bf16[256,1024]{1,0:T(8,128)(2,1)}, bf16[256,1024]{1,0:T(8,128)(2,1)S(1)}, u32[]{:S(2)}, u32[]{:S(2)}) %collective-permute-start) | collective-permute-done | bytes 524320 | tf_op jit(solution)/shard_map/while/body/eval_jaxpr/ppermute | solution.py:32
  373.4 11.1 %collective-permute-done = bf16[256,1024]{1,0:T(8,128)(2,1)S(1)} collective-permute-done((bf16[256,1024]{1,0:T(8,128)(2,1)}, bf16[256,1024]{1,0:T(8,128)(2,1)S(1)}, u32[]{:S(2)}, u32[]{:S(2)}) %collective-permute-start) | collective-permute-done | bytes 524320 | tf_op jit(solution)/shard_map/while/body/eval_jaxpr/ppermute | solution.py:32
  391.8 11.1 %collective-permute-done = bf16[256,1024]{1,0:T(8,128)(2,1)S(1)} collective-permute-done((bf16[256,1024]{1,0:T(8,128)(2,1)}, bf16[256,1024]{1,0:T(8,128)(2,1)S(1)}, u32[]{:S(2)}, u32[]{:S(2)}) %collective-permute-start) | collective-permute-done | bytes 524320 | tf_op jit(solution)/shard_map/while/body/eval_jaxpr/ppermute | solution.py:32
  410.2 11.1 %collective-permute-done = bf16[256,1024]{1,0:T(8,128)(2,1)S(1)} collective-permute-done((bf16[256,1024]{1,0:T(8,128)(2,1)}, bf16[256,1024]{1,0:T(8,128)(2,1)S(1)}, u32[]{:S(2)}, u32[]{:S(2)}) %collective-permute-start) | collective-permute-done | bytes 524320 | tf_op jit(solution)/shard_map/while/body/eval_jaxpr/ppermute | solution.py:32
  428.6 11.1 %collective-permute-done = bf16[256,1024]{1,0:T(8,128)(2,1)S(1)} collective-permute-done((bf16[256,1024]{1,0:T(8,128)(2,1)}, bf16[256,1024]{1,0:T(8,128)(2,1)S(1)}, u32[]{:S(2)}, u32[]{:S(2)}) %collective-permute-start) | collective-permute-done | bytes 524320 | tf_op jit(solution)/shard_map/while/body/eval_jaxpr/ppermute | solution.py:32
  447.1 11.1 %collective-permute-done = bf16[256,1024]{1,0:T(8,128)(2,1)S(1)} collective-permute-done((bf16[256,1024]{1,0:T(8,128)(2,1)}, bf16[256,1024]{1,0:T(8,128)(2,1)S(1)}, u32[]{:S(2)}, u32[]{:S(2)}) %collective-permute-start) | collective-permute-done | bytes 524320 | tf_op jit(solution)/shard_map/while/body/eval_jaxpr/ppermute | solution.py:32
  465.5 11.1 %collective-permute-done = bf16[256,1024]{1,0:T(8,128)(2,1)S(1)} collective-permute-done((bf16[256,1024]{1,0:T(8,128)(2,1)}, bf16[256,1024]{1,0:T(8,128)(2,1)S(1)}, u32[]{:S(2)}, u32[]{:S(2)}) %collective-permute-start) | collective-permute-done | bytes 524320 | tf_op jit(solution)/shard_map/while/body/eval_jaxpr/ppermute | solution.py:32
  483.9 11.1 %collective-permute-done = bf16[256,1024]{1,0:T(8,128)(2,1)S(1)} collective-permute-done((bf16[256,1024]{1,0:T(8,128)(2,1)}, bf16[256,1024]{1,0:T(8,128)(2,1)S(1)}, u32[]{:S(2)}, u32[]{:S(2)}) %collective-permute-start) | collective-permute-done | bytes 524320 | tf_op jit(solution)/shard_map/while/body/eval_jaxpr/ppermute | solution.py:32
  502.3 11.1 %collective-permute-done = bf16[256,1024]{1,0:T(8,128)(2,1)S(1)} collective-permute-done((bf16[256,1024]{1,0:T(8,128)(2,1)}, bf16[256,1024]{1,0:T(8,128)(2,1)S(1)}, u32[]{:S(2)}, u32[]{:S(2)}) %collective-permute-start) | collective-permute-done | bytes 524320 | tf_op jit(solution)/shard_map/while/body/eval_jaxpr/ppermute | solution.py:32
  520.8 11.1 %collective-permute-done = bf16[256,1024]{1,0:T(8,128)(2,1)S(1)} collective-permute-done((bf16[256,1024]{1,0:T(8,128)(2,1)}, bf16[256,1024]{1,0:T(8,128)(2,1)S(1)}, u32[]{:S(2)}, u32[]{:S(2)}) %collective-permute-start) | collective-permute-done | bytes 524320 | tf_op jit(solution)/shard_map/while/body/eval_jaxpr/ppermute | solution.py:32
  539.2 11.1 %collective-permute-done = bf16[256,1024]{1,0:T(8,128)(2,1)S(1)} collective-permute-done((bf16[256,1024]{1,0:T(8,128)(2,1)}, bf16[256,1024]{1,0:T(8,128)(2,1)S(1)}, u32[]{:S(2)}, u32[]{:S(2)}) %collective-permute-start) | collective-permute-done | bytes 524320 | tf_op jit(solution)/shard_map/while/body/eval_jaxpr/ppermute | solution.py:32
  557.6 11.1 %collective-permute-done = bf16[256,1024]{1,0:T(8,128)(2,1)S(1)} collective-permute-done((bf16[256,1024]{1,0:T(8,128)(2,1)}, bf16[256,1024]{1,0:T(8,128)(2,1)S(1)}, u32[]{:S(2)}, u32[]{:S(2)}) %collective-permute-start) | collective-permute-done | bytes 524320 | tf_op jit(solution)/shard_map/while/body/eval_jaxpr/ppermute | solution.py:32
  576.0 11.1 %collective-permute-done = bf16[256,1024]{1,0:T(8,128)(2,1)S(1)} collective-permute-done((bf16[256,1024]{1,0:T(8,128)(2,1)}, bf16[256,1024]{1,0:T(8,128)(2,1)S(1)}, u32[]{:S(2)}, u32[]{:S(2)}) %collective-permute-start) | collective-permute-done | bytes 524320 | tf_op jit(solution)/shard_map/while/body/eval_jaxpr/ppermute | solution.py:32
  594.5 11.1 %collective-permute-done = bf16[256,1024]{1,0:T(8,128)(2,1)S(1)} collective-permute-done((bf16[256,1024]{1,0:T(8,128)(2,1)}, bf16[256,1024]{1,0:T(8,128)(2,1)S(1)}, u32[]{:S(2)}, u32[]{:S(2)}) %collective-permute-start) | collective-permute-done | bytes 524320 | tf_op jit(solution)/shard_map/while/body/eval_jaxpr/ppermute | solution.py:32
  (625 shorter events, 127.9 us)
Async XLA Ops:
  0.6 301.2 %copy-start = (bf16[1,256,2048]{2,1,0:T(8,128)(2,1)S(1)}, bf16[1,256,2048]{2,1,0:T(8,128)(2,1)}, u32[]{:S(2)}) copy-start(bf16[1,256,2048]{2,1,0:T(8,128)(2,1)} %param.9) | copy-start | bytes 3145732
  8.6 15.3 %copy-start.10 = (s32[16]{0:T(128)S(1)}, s32[16]{0:T(128)}, u32[]{:S(2)}) copy-start(s32[16]{0:T(128)} %param.11) | copy-start | bytes 196
  8.6 16.5 %copy-start.9 = (s32[1,256]{1,0:T(1,128)S(1)}, s32[1,256]{1,0:T(1,128)}, u32[]{:S(2)}) copy-start(s32[1,256]{1,0:T(1,128)} %param.10) | copy-start | bytes 3076
  8.6 18.9 %copy-start.11 = (u32[256]{0:T(256)S(1)}, u32[256]{0:T(256)}, u32[]{:S(2)}) copy-start(u32[256]{0:T(256)} %constant.170) | copy-start | bytes 3076
  8.6 293.3 %all-to-all-start = ((bf16[256,8,3072]{2,1,0:T(8,128)(2,1)}), bf16[256,8,3072]{2,1,0:T(8,128)(2,1)}, u32[]{:S(2)}, u32[]{:S(2)}) async-start(bf16[256,8,3072]{2,1,0:T(8,128)(2,1)} %stack.2), calls=%async_computation | async-start | bytes 25165824 | tf_op jit(solution)/shard_map/all_to_all | solution.py:23
  335.1 12.4 %collective-permute-start = (bf16[256,1024]{1,0:T(8,128)(2,1)}, bf16[256,1024]{1,0:T(8,128)(2,1)S(1)}, u32[]{:S(2)}, u32[]{:S(2)}) collective-permute-start(bf16[256,1024]{1,0:T(8,128)(2,1)} %get-tuple-element.873), channel_id=1, source_target_pairs={{0,1},{1,2},{2,3},{3,4},{4,5},{5,6},{6,7},{7,8},{8,9},{9,10},{10,1... | collective-permute-start | bytes 1572872 | tf_op jit(solution)/shard_map/while/body/eval_jaxpr/ppermute | solution.py:32
  353.6 12.4 %collective-permute-start = (bf16[256,1024]{1,0:T(8,128)(2,1)}, bf16[256,1024]{1,0:T(8,128)(2,1)S(1)}, u32[]{:S(2)}, u32[]{:S(2)}) collective-permute-start(bf16[256,1024]{1,0:T(8,128)(2,1)} %get-tuple-element.873), channel_id=1, source_target_pairs={{0,1},{1,2},{2,3},{3,4},{4,5},{5,6},{6,7},{7,8},{8,9},{9,10},{10,1... | collective-permute-start | bytes 1572872 | tf_op jit(solution)/shard_map/while/body/eval_jaxpr/ppermute | solution.py:32
  372.0 12.4 %collective-permute-start = (bf16[256,1024]{1,0:T(8,128)(2,1)}, bf16[256,1024]{1,0:T(8,128)(2,1)S(1)}, u32[]{:S(2)}, u32[]{:S(2)}) collective-permute-start(bf16[256,1024]{1,0:T(8,128)(2,1)} %get-tuple-element.873), channel_id=1, source_target_pairs={{0,1},{1,2},{2,3},{3,4},{4,5},{5,6},{6,7},{7,8},{8,9},{9,10},{10,1... | collective-permute-start | bytes 1572872 | tf_op jit(solution)/shard_map/while/body/eval_jaxpr/ppermute | solution.py:32
  390.4 12.4 %collective-permute-start = (bf16[256,1024]{1,0:T(8,128)(2,1)}, bf16[256,1024]{1,0:T(8,128)(2,1)S(1)}, u32[]{:S(2)}, u32[]{:S(2)}) collective-permute-start(bf16[256,1024]{1,0:T(8,128)(2,1)} %get-tuple-element.873), channel_id=1, source_target_pairs={{0,1},{1,2},{2,3},{3,4},{4,5},{5,6},{6,7},{7,8},{8,9},{9,10},{10,1... | collective-permute-start | bytes 1572872 | tf_op jit(solution)/shard_map/while/body/eval_jaxpr/ppermute | solution.py:32
  408.8 12.4 %collective-permute-start = (bf16[256,1024]{1,0:T(8,128)(2,1)}, bf16[256,1024]{1,0:T(8,128)(2,1)S(1)}, u32[]{:S(2)}, u32[]{:S(2)}) collective-permute-start(bf16[256,1024]{1,0:T(8,128)(2,1)} %get-tuple-element.873), channel_id=1, source_target_pairs={{0,1},{1,2},{2,3},{3,4},{4,5},{5,6},{6,7},{7,8},{8,9},{9,10},{10,1... | collective-permute-start | bytes 1572872 | tf_op jit(solution)/shard_map/while/body/eval_jaxpr/ppermute | solution.py:32
  423.4 1.4 copy-start.1
  427.3 12.4 %collective-permute-start = (bf16[256,1024]{1,0:T(8,128)(2,1)}, bf16[256,1024]{1,0:T(8,128)(2,1)S(1)}, u32[]{:S(2)}, u32[]{:S(2)}) collective-permute-start(bf16[256,1024]{1,0:T(8,128)(2,1)} %get-tuple-element.873), channel_id=1, source_target_pairs={{0,1},{1,2},{2,3},{3,4},{4,5},{5,6},{6,7},{7,8},{8,9},{9,10},{10,1... | collective-permute-start | bytes 1572872 | tf_op jit(solution)/shard_map/while/body/eval_jaxpr/ppermute | solution.py:32
  445.7 12.4 %collective-permute-start = (bf16[256,1024]{1,0:T(8,128)(2,1)}, bf16[256,1024]{1,0:T(8,128)(2,1)S(1)}, u32[]{:S(2)}, u32[]{:S(2)}) collective-permute-start(bf16[256,1024]{1,0:T(8,128)(2,1)} %get-tuple-element.873), channel_id=1, source_target_pairs={{0,1},{1,2},{2,3},{3,4},{4,5},{5,6},{6,7},{7,8},{8,9},{9,10},{10,1... | collective-permute-start | bytes 1572872 | tf_op jit(solution)/shard_map/while/body/eval_jaxpr/ppermute | solution.py:32
  464.1 12.4 %collective-permute-start = (bf16[256,1024]{1,0:T(8,128)(2,1)}, bf16[256,1024]{1,0:T(8,128)(2,1)S(1)}, u32[]{:S(2)}, u32[]{:S(2)}) collective-permute-start(bf16[256,1024]{1,0:T(8,128)(2,1)} %get-tuple-element.873), channel_id=1, source_target_pairs={{0,1},{1,2},{2,3},{3,4},{4,5},{5,6},{6,7},{7,8},{8,9},{9,10},{10,1... | collective-permute-start | bytes 1572872 | tf_op jit(solution)/shard_map/while/body/eval_jaxpr/ppermute | solution.py:32
  482.5 12.4 %collective-permute-start = (bf16[256,1024]{1,0:T(8,128)(2,1)}, bf16[256,1024]{1,0:T(8,128)(2,1)S(1)}, u32[]{:S(2)}, u32[]{:S(2)}) collective-permute-start(bf16[256,1024]{1,0:T(8,128)(2,1)} %get-tuple-element.873), channel_id=1, source_target_pairs={{0,1},{1,2},{2,3},{3,4},{4,5},{5,6},{6,7},{7,8},{8,9},{9,10},{10,1... | collective-permute-start | bytes 1572872 | tf_op jit(solution)/shard_map/while/body/eval_jaxpr/ppermute | solution.py:32
  501.0 12.4 %collective-permute-start = (bf16[256,1024]{1,0:T(8,128)(2,1)}, bf16[256,1024]{1,0:T(8,128)(2,1)S(1)}, u32[]{:S(2)}, u32[]{:S(2)}) collective-permute-start(bf16[256,1024]{1,0:T(8,128)(2,1)} %get-tuple-element.873), channel_id=1, source_target_pairs={{0,1},{1,2},{2,3},{3,4},{4,5},{5,6},{6,7},{7,8},{8,9},{9,10},{10,1... | collective-permute-start | bytes 1572872 | tf_op jit(solution)/shard_map/while/body/eval_jaxpr/ppermute | solution.py:32
  519.4 12.4 %collective-permute-start = (bf16[256,1024]{1,0:T(8,128)(2,1)}, bf16[256,1024]{1,0:T(8,128)(2,1)S(1)}, u32[]{:S(2)}, u32[]{:S(2)}) collective-permute-start(bf16[256,1024]{1,0:T(8,128)(2,1)} %get-tuple-element.873), channel_id=1, source_target_pairs={{0,1},{1,2},{2,3},{3,4},{4,5},{5,6},{6,7},{7,8},{8,9},{9,10},{10,1... | collective-permute-start | bytes 1572872 | tf_op jit(solution)/shard_map/while/body/eval_jaxpr/ppermute | solution.py:32
  533.9 1.4 copy-start.1
  537.8 12.4 %collective-permute-start = (bf16[256,1024]{1,0:T(8,128)(2,1)}, bf16[256,1024]{1,0:T(8,128)(2,1)S(1)}, u32[]{:S(2)}, u32[]{:S(2)}) collective-permute-start(bf16[256,1024]{1,0:T(8,128)(2,1)} %get-tuple-element.873), channel_id=1, source_target_pairs={{0,1},{1,2},{2,3},{3,4},{4,5},{5,6},{6,7},{7,8},{8,9},{9,10},{10,1... | collective-permute-start | bytes 1572872 | tf_op jit(solution)/shard_map/while/body/eval_jaxpr/ppermute | solution.py:32
  556.2 12.4 %collective-permute-start = (bf16[256,1024]{1,0:T(8,128)(2,1)}, bf16[256,1024]{1,0:T(8,128)(2,1)S(1)}, u32[]{:S(2)}, u32[]{:S(2)}) collective-permute-start(bf16[256,1024]{1,0:T(8,128)(2,1)} %get-tuple-element.873), channel_id=1, source_target_pairs={{0,1},{1,2},{2,3},{3,4},{4,5},{5,6},{6,7},{7,8},{8,9},{9,10},{10,1... | collective-permute-start | bytes 1572872 | tf_op jit(solution)/shard_map/while/body/eval_jaxpr/ppermute | solution.py:32
  574.7 12.4 %collective-permute-start = (bf16[256,1024]{1,0:T(8,128)(2,1)}, bf16[256,1024]{1,0:T(8,128)(2,1)S(1)}, u32[]{:S(2)}, u32[]{:S(2)}) collective-permute-start(bf16[256,1024]{1,0:T(8,128)(2,1)} %get-tuple-element.873), channel_id=1, source_target_pairs={{0,1},{1,2},{2,3},{3,4},{4,5},{5,6},{6,7},{7,8},{8,9},{9,10},{10,1... | collective-permute-start | bytes 1572872 | tf_op jit(solution)/shard_map/while/body/eval_jaxpr/ppermute | solution.py:32
  593.1 12.4 %collective-permute-start = (bf16[256,1024]{1,0:T(8,128)(2,1)}, bf16[256,1024]{1,0:T(8,128)(2,1)S(1)}, u32[]{:S(2)}, u32[]{:S(2)}) collective-permute-start(bf16[256,1024]{1,0:T(8,128)(2,1)} %get-tuple-element.873), channel_id=1, source_target_pairs={{0,1},{1,2},{2,3},{3,4},{4,5},{5,6},{6,7},{7,8},{8,9},{9,10},{10,1... | collective-permute-start | bytes 1572872 | tf_op jit(solution)/shard_map/while/body/eval_jaxpr/ppermute | solution.py:32
  611.5 1.7 copy-start.6
  611.5 2.2 copy-start.3
  (88 other events, 91.5 us)
